TPU v7x, 512 devices: a whole 4x8x8 slice. The times are simulated.
512 devices in a mesh: xy: 128 (over x, y_hi, z, core), gz: 4 (over y_lo).
Axes of the slice: x: 4, y: 8 (y_hi: 2, y_lo: 4; y = y_hi * 4 + y_lo), z: 8, core: 2. Of those that a mesh axis runs over, the one named last changes fastest.
Arguments:
- density: float32 [16384, 2048], P('xy', 'gz'), may hold values from 0 to 1
- cotangent: float32 [6, 16, 2048, 256], P(None, 'gz', 'xy'), may hold values from -6 to 6
- slope: int32 [16], P('gz'), may hold values from 0 to 4
- layer_block: int32 [16], P('gz'), may hold values from 0 to 3
- block_eps: float32 [4, 2], replicated, may hold values from 1.5 to 12
Outputs:
- grad_filtered: float32 [16384, 2048], P('xy', 'gz')
- grad_density: float32 [16384, 2048], P('xy', 'gz')
All inputs are finite; a program needn't handle non-finite values.
Results may differ from a plain program's by a relative error of at most 0.0003.
Values sent between devices are 32-bit elements; how exact they have to be, the bound alone decides.
No kernel may reach another device: no remote copies, remote signals or barrier semaphores. Data moves between devices by JAX's collectives and lax.ppermute only.
A program may use at most 64 MiB of HBM per device.

v0:
```python
import math

import jax
import jax.numpy as jnp
from jax import lax
from jax.experimental import pallas as pl
from jax.experimental.pallas import tpu as pltpu
from jax.sharding import PartitionSpec as P

SUB = 8
RADIUS = 32
SLOPES = 5
SCALE = 1.0 / float((RADIUS + 1) ** 2)
BF = jnp.bfloat16
F32 = jnp.float32
VMEM = pl.BlockSpec(memory_space=pltpu.VMEM)
SMEM = pl.BlockSpec(memory_space=pltpu.SMEM)
HBM = pl.BlockSpec(memory_space=pltpu.HBM)
LIMIT = 24 << 20

HEIGHT = 128
WIDTH = 512
WIDE = WIDTH + 2 * RADIUS
CELLS = WIDE // SUB
ROWS = 224


def iota(shape, dim):
    return lax.broadcasted_iota(jnp.int32, shape, dim)


def parts_of(value, count):
    parts = []
    for index in range(count):
        part = value.astype(BF)
        parts.append(part)
        if index + 1 < count:
            value = value - part.astype(F32)
    return parts


def band(rows, cols):
    offset = iota((rows, cols), 1) - iota((rows, cols), 0) - RADIUS
    return jnp.maximum(RADIUS + 1 - jnp.abs(offset), 0).astype(F32).astype(BF)


def dot(a, b):
    return jnp.dot(a, b, preferred_element_type=F32)


def place_lanes():
    return (iota((1, HEIGHT), 1) % SUB).astype(F32) - 3.5


def call(body, outs, scratch, flops, moved, *args, smem=()):
    return pl.pallas_call(
        body,
        out_shape=[out if hasattr(out, "dtype") else jax.ShapeDtypeStruct(out, F32) for out in outs],
        in_specs=[SMEM if index in smem else VMEM for index in range(len(args))],
        out_specs=[VMEM for _ in outs],
        scratch_shapes=[pltpu.VMEM(shape, F32) for shape in scratch],
        compiler_params=pltpu.CompilerParams(vmem_limit_bytes=LIMIT),
        cost_estimate=pl.CostEstimate(flops=flops, bytes_accessed=moved, transcendentals=0),
    )(*args)


def pack_body(slope_hbm, block_hbm, eps_hbm, cot_hbm, send_hbm, slope, block, eps, cot, send, sems):
    small = [
        pltpu.make_async_copy(source, target, sems.at[3 + index])
        for index, (source, target) in enumerate([(slope_hbm, slope), (block_hbm, block), (eps_hbm, eps)])
    ]
    slabs = [
        pltpu.make_async_copy(cot_hbm.at[pl.ds(128 * slab, 128)], cot.at[pl.ds(128 * slab, 128)], sems.at[slab])
        for slab in range(3)
    ]
    for copy in slabs + small:
        copy.start()
    low = iota((SUB, HEIGHT), 0) < 4
    zero = jnp.zeros((SUB, HEIGHT), F32)
    outs = []

    def put(first, rows):
        copy = pltpu.make_async_copy(
            send.at[:, pl.ds(first, rows)], send_hbm.at[:, pl.ds(first, rows)], sems.at[6 + len(outs)]
        )
        copy.start()
        outs.append(copy)

    for slab in range(3):
        slabs[slab].wait()
        turned = cot[slab * 128 : slab * 128 + 128, :].T
        for owner in range(4):
            first, base = (64 * owner, 72 * slab)
            send[owner, base : base + 64, :] = turned[first : first + 64]
            after = zero if owner == 3 else turned[first + 64 : first + 72]
            before = zero if owner == 0 else turned[first - 8 : first]
            send[owner, base + 64 : base + 72, :] = jnp.where(low, after, before)
        if slab < 2:
            put(72 * slab, 72)
    for copy in small:
        copy.wait()
    layer = (iota((SUB, HEIGHT), 1) % 64) // 16
    row = iota((SUB, HEIGHT), 0)
    table = zero
    for index in range(4):
        one = eps[0, block[index]]
        two = eps[1, block[index]]
        level = slope[index].astype(F32)
        column = jnp.where(row == 0, level, jnp.where(row == 1, one, jnp.where(row == 2, two, 0.0)))
        table = jnp.where(layer == index, column, table)
    for owner in range(4):
        send[owner, 216:224, :] = table
    put(144, 80)
    for copy in outs:
        copy.wait()


def odd(axis):
    return lax.rem(lax.axis_index(axis), 2) == 1


def sides(axis, near, far):
    return (jnp.where(odd(axis), near, far), jnp.where(odd(axis), far, near))


def low_lanes():
    return iota((1, 128), 1) < 64


def columns_body(density, to_near, to_far, rows_near, rows_far, begin, end, sems):
    first = jnp.where(odd("xy"), 0, HEIGHT - RADIUS)
    moves = [
        (density.at[:, pl.ds(0, 128)], begin),
        (density.at[:, pl.ds(WIDTH - 128, 128)], end),
        (density.at[pl.ds(pl.multiple_of(first, RADIUS), RADIUS)], rows_near),
        (density.at[pl.ds(pl.multiple_of(HEIGHT - RADIUS - first, RADIUS), RADIUS)], rows_far),
    ]
    copies = [pltpu.make_async_copy(source, target, sems.at[index]) for index, (source, target) in enumerate(moves)]
    for copy in copies:
        copy.start()
    copies[0].wait()
    copies[1].wait()
    first = jnp.where(low_lanes(), begin[:64, :], pltpu.roll(begin[64:, :], 64, 1))
    last = jnp.where(low_lanes(), pltpu.roll(end[:64, :], 64, 1), end[64:, :])
    to_near[...], to_far[...] = sides("gz", first, last)
    copies[2].wait()
    copies[3].wait()


def edges_body(near, far, rows_near, rows_far, halo, to_near, to_far):
    before, after = sides("gz", near[...], far[...])
    halo[:64] = jnp.where(low_lanes(), after, pltpu.roll(before, 64, 1))
    halo[64:] = jnp.where(low_lanes(), pltpu.roll(after, 64, 1), before)
    first, last = (slice(0, RADIUS), slice(HEIGHT - RADIUS, HEIGHT))
    to_near[:, :WIDTH] = rows_near[...]
    to_far[:, :WIDTH] = rows_far[...]
    to_near[:, WIDTH:], to_far[:, WIDTH:] = sides("xy", halo[first, :], halo[last, :])


def prior_body(own, halo, start, across, ahead, plain, pool, spread):
    middle = jnp.concatenate([own[...], halo[...]], axis=1)
    matrix = band(HEIGHT, HEIGHT + 2 * RADIUS)[:, RADIUS : RADIUS + HEIGHT]
    total = None
    for part in parts_of(middle, 3):
        term = dot(matrix, part)
        total = term if total is None else total + term
    turned = total.T
    padded = jnp.concatenate([turned[WIDTH + 64 :], turned[: WIDTH + 64]], axis=0)
    padded = jnp.concatenate(parts_of(padded, 3), axis=1)
    matrix = band(192, 256)
    plain[...] = matrix
    for block in range(3):
        wide = dot(matrix, padded[192 * block : 192 * block + 256])
        keep(start, block, wide[:, :128] + wide[:, 128:256] + wide[:, 256:])
    offset = iota((384, 192), 0) - iota((384, 192), 1) - 3 * RADIUS
    across[...] = jnp.maximum(RADIUS + 1 - jnp.abs(offset), 0).astype(F32).astype(BF)
    row = iota((HEIGHT, 192), 1) % 64
    offset = row + jnp.where(row < RADIUS, -RADIUS, 3 * RADIUS) - iota((HEIGHT, 192), 0)
    ahead[...] = jnp.maximum(RADIUS + 1 - jnp.abs(offset), 0).astype(F32).astype(BF)
    base = (iota((128, 256), 0) // SUB == iota((128, 256), 1) % 16).astype(F32).astype(BF)
    pool[...] = jnp.concatenate([base, base], axis=0)
    spread[...] = (iota((256, HEIGHT), 0) % 16 == iota((256, HEIGHT), 1) // SUB).astype(F32).astype(BF)


def places(block):
    first = 192 * block - RADIUS
    return [(0, RADIUS, WIDTH + RADIUS), (RADIUS, 192, 0)] if block == 0 else [(0, 192, first)]


def keep(target, block, value):
    for begin, end, first in places(block):
        target[first : first + end - begin, :] = value[begin:end]


def forward(near, down, up, start, across, ahead, pool, slopes, pooled, natural):
    before, after = sides("xy", near[...], jnp.where(odd("xy"), up[...], down[...]))
    rows = jnp.concatenate(parts_of(jnp.concatenate([before, after], axis=0), 3), axis=0)
    windows = [jnp.concatenate([rows[:, WIDTH:], rows[:, :256]], axis=1), rows[:, 128:384], rows[:, 256:]]
    for block, window in enumerate(windows):
        weights = across[64:320, :] if block == 1 else across[...]
        wide = dot(window, weights)
        beside = parts_of(wide[:64] + wide[64:128] + wide[128:], 3)
        added = dot(ahead[...], jnp.concatenate(beside, axis=0)).T
        own = jnp.concatenate([start[first : first + end - begin, :] for begin, end, first in places(block)], axis=0)
        keep(natural, block, jnp.exp(16.0 - (32.0 * SCALE * SCALE) * (own + added)))
    expo = [natural[pl.ds(q, CELLS, stride=SUB), :] for q in range(SUB)]
    place = place_lanes()
    stacks = []
    for s in range(SLOPES):
        factor = math.exp(0.64 * (s - 2))
        mean, slant = (None, None)
        for q in range(SUB // 2):
            pair = []
            for row in (q, SUB - 1 - q):
                scaled = factor * expo[row]
                fill = 1.0 / (1.0 + scaled)
                slopes[s, row] = fill * fill * scaled
                pair.append(fill)
            both, apart = (pair[0] + pair[1], (3.5 - q) * (pair[1] - pair[0]))
            mean = both if mean is None else mean + both
            slant = apart if slant is None else slant + apart
        stacks += [mean, mean * place, slant]
    stacks.append(jnp.zeros((SUB, HEIGHT), F32))
    rows = jnp.concatenate(parts_of(jnp.concatenate(stacks, axis=0), 2), axis=1)
    pooled[...] = dot(rows, pool[...])


def adjoint_body(near, down, up, got, start, across, ahead, plain, pool, spread, out, turned, to_near, to_far, slopes, pooled, natural):
    forward(near, down, up, start, across, ahead, pool, slopes, pooled, natural)
    half = low_lanes()

    def pair(a, b):
        return jnp.where(half, a, b)

    def line(row):
        value = [got[g, row : row + 1, :] for g in range(4)]
        return jnp.concatenate([pair(value[0], value[1]), pair(value[2], value[3])], axis=1)

    level, eps_one, eps_two = (line(216), line(217), line(218))
    comps = []
    for slab in range(3):
        value = [got[g, 72 * slab : 72 * slab + 72, :] for g in range(4)]
        swapped = [pltpu.roll(v, 64, 1) for v in value]
        comps.append(jnp.concatenate([pair(value[0], swapped[1]), pair(value[2], swapped[3])], axis=1))
        comps.append(jnp.concatenate([pair(swapped[0], value[1]), pair(swapped[2], value[3])], axis=1))
    cxx, cyy, czz, cxy, cxz, cyz = comps
    frac = jnp.zeros((CELLS, 256), F32)
    grad_x = jnp.zeros((CELLS, 256), F32)
    grad_y = jnp.zeros((CELLS, 256), F32)
    masks = []
    for s in range(SLOPES):
        mask = level == float(s)
        masks.append(mask)
        frac = jnp.where(mask, pooled[216 * s : 216 * s + 72, :], frac)
        grad_x = jnp.where(mask, pooled[216 * s + 72 : 216 * s + 144, :], grad_x)
        grad_y = jnp.where(mask, pooled[216 * s + 144 : 216 * s + 216, :], grad_y)
    frac, grad_x, grad_y = (value * (1.0 / 64.0) for value in (frac, grad_x, grad_y))
    lift = 0.2 * (1.0 + level)
    slope_mean = eps_one - eps_two
    inv_two = 1.0 / eps_two
    slope_inv = 1.0 / eps_one - inv_two
    mean_eps = eps_two + frac * slope_mean
    harmonic = 1.0 / (inv_two + frac * slope_inv)
    inv_norm = 1.0 / (grad_x * grad_x + grad_y * grad_y + lift * lift)
    weight = (harmonic - mean_eps) * inv_norm
    along_x = cxx * grad_x + cxy * grad_y + cxz * lift
    along_y = cyy * grad_y + cyz * lift
    quad = grad_x * along_x + grad_y * along_y + czz * (lift * lift)
    trace = cxx + cyy + czz
    d_frac = trace * slope_mean - quad * inv_norm * (harmonic * harmonic * slope_inv + slope_mean)
    shared = 2.0 * inv_norm * quad
    d_x = weight * (along_x + cxx * grad_x - grad_x * shared)
    d_y = weight * (along_y + cyy * grad_y + cxy * grad_x - grad_y * shared)
    stack = jnp.concatenate([d_frac, d_x, d_y, jnp.zeros((SUB, 256), F32)], axis=0) * 0.5
    high, low = parts_of(stack, 2)
    place = place_lanes()
    flat, tilt = ([], [])
    for mask in masks:
        chosen = jnp.where(mask, 1.0, 0.0).astype(BF)
        both = dot(high * chosen, spread[...]) + dot(low * chosen, spread[...])
        flat.append(both[:72] + place * both[72:144])
        tilt.append(both[144:216])
    for q in range(SUB // 2):
        up, down = (None, None)
        for s in range(SLOPES):
            lean = (3.5 - q) * tilt[s]
            one, two = (slopes[s, q] * (flat[s] - lean), slopes[s, SUB - 1 - q] * (flat[s] + lean))
            up, down = (one, two) if up is None else (up + one, down + two)
        natural[pl.ds(q, CELLS, stride=SUB), :] = up
        natural[pl.ds(SUB - 1 - q, CELLS, stride=SUB), :] = down
    out[...] = natural[:WIDTH, :]
    pieces = []
    for block in range(3):
        count = 192 if block < 2 else 128
        if block == 0:
            window = jnp.concatenate([natural[WIDTH + RADIUS : WIDE, :], natural[:224, :]], axis=0)
        else:
            window = natural[192 * block - RADIUS : 192 * block + count + RADIUS, :]
        wide = dot(plain[:count, : count + 64], jnp.concatenate(parts_of(window, 2), axis=1))
        pieces.append((wide[:, :128] + wide[:, 128:]) * SCALE)
    result = jnp.concatenate(pieces, axis=0).T
    turned[...] = result
    to_near[...], to_far[...] = sides("xy", result[:RADIUS], result[HEIGHT - RADIUS :])


def emit_odd(grad, turned, out, result, partial, *scratch):
    @pl.when(odd("xy"))
    def _():
        emit(grad, turned, out, result, partial, *scratch)


def emit_even(grad, turned, out_before, result_before, out, result, partial, *scratch):
    @pl.when(jnp.logical_not(odd("xy")))
    def _():
        emit(grad, turned, out, result, partial, *scratch)


def emit(grad, turned, out, result, partial, whole, middle, sems):
    whole[...] = grad[...].T
    copies = [pltpu.make_async_copy(whole, out, sems.at[0])]
    copies[0].start()
    matrix = band(HEIGHT, HEIGHT + 2 * RADIUS)[:, RADIUS : RADIUS + HEIGHT]
    high, low = parts_of(turned[...], 2)
    total = (dot(matrix, high) + dot(matrix, low)) * SCALE
    middle[...] = total[RADIUS : HEIGHT - RADIUS]
    copies.append(pltpu.make_async_copy(middle, result.at[pl.ds(RADIUS, HEIGHT - 2 * RADIUS)], sems.at[1]))
    copies[1].start()
    partial[:RADIUS] = total[:RADIUS]
    partial[RADIUS:] = total[HEIGHT - RADIUS :]
    for copy in copies:
        copy.wait()


def last_body(near, far, partial_odd, partial_even, start, result, ends, sems):
    partial = jnp.where(odd("xy"), partial_odd[...], partial_even[...])
    before, after = sides("xy", near[...], far[...])
    matrix = band(RADIUS, 3 * RADIUS)
    copies = []
    for index, (rows, weights) in enumerate([(before, matrix[:, :RADIUS]), (after, matrix[:, 2 * RADIUS :])]):
        high, low = parts_of(rows, 2)
        ends[index] = partial[RADIUS * index : RADIUS * (index + 1)] + (dot(weights, high) + dot(weights, low)) * SCALE
        where = result.at[pl.ds((HEIGHT - RADIUS) * index, RADIUS)]
        copies.append(pltpu.make_async_copy(ends.at[index], where, sems.at[index]))
        copies[-1].start()
    for copy in copies:
        copy.wait()


def pairs(axis, start):
    return [(i, i + 1) for i in range(start, lax.axis_size(axis) - 1, 2)]


def back(steps):
    return [(j, i) for i, j in steps]


def swap(near, far, axis):
    inner, outer = (pairs(axis, 0), pairs(axis, 1))
    far = lax.ppermute(far, axis, outer + back(outer))
    return (lax.ppermute(near, axis, inner + back(inner)), far)


def steps(density, cotangent, slope, layer_block, block_eps):
    shapes = [(64, 128), (64, 128), (RADIUS, WIDTH), (RADIUS, WIDTH)]
    near, far, *rows = pl.pallas_call(
        columns_body,
        name="columns",
        out_shape=[jax.ShapeDtypeStruct(shape, F32) for shape in shapes],
        in_specs=[HBM],
        out_specs=[VMEM] * 4,
        scratch_shapes=[pltpu.VMEM((HEIGHT, 128), F32), pltpu.VMEM((HEIGHT, 128), F32), pltpu.SemaphoreType.DMA((4,))],
        compiler_params=pltpu.CompilerParams(vmem_limit_bytes=8 << 20),
        cost_estimate=pl.CostEstimate(flops=10**6, bytes_accessed=10**6, transcendentals=0),
    )(pltpu.with_memory_space_constraint(density, pltpu.HBM))
    near, far = swap(near, far, "gz")
    (send,) = pl.pallas_call(
        pack_body,
        name="pack",
        out_shape=[jax.ShapeDtypeStruct((4, ROWS, 128), F32)],
        in_specs=[HBM] * 4,
        out_specs=[HBM],
        scratch_shapes=[
            pltpu.SMEM((4,), jnp.int32),
            pltpu.SMEM((4,), jnp.int32),
            pltpu.SMEM((2, 4), F32),
            pltpu.VMEM((384, 256), F32),
            pltpu.VMEM((4, ROWS, 128), F32),
            pltpu.SemaphoreType.DMA((9,)),
        ],
        compiler_params=pltpu.CompilerParams(vmem_limit_bytes=60 * 1024 * 1024),
        cost_estimate=pl.CostEstimate(flops=10**6, bytes_accessed=10**6, transcendentals=0),
    )(slope, layer_block, block_eps.T, cotangent.reshape(384, 256))
    got = lax.all_to_all(send, "gz", 0, 0, tiled=True)
    edges = [(HEIGHT, 128), (RADIUS, WIDTH + 128), (RADIUS, WIDTH + 128)]
    halo, near, far = call(edges_body, edges, [], 10**5, 10**6, near, far, *rows)
    inner, outer = (pairs("xy", 0), pairs("xy", 1))
    down = lax.ppermute(far, "xy", outer)
    up = lax.ppermute(far, "xy", back(outer))
    near = lax.ppermute(near, "xy", inner + back(inner))
    shapes = [(WIDTH, HEIGHT), (HEIGHT, WIDTH), (RADIUS, WIDTH), (RADIUS, WIDTH)]
    scratch = [(SLOPES, SUB, CELLS, HEIGHT), (1088, 256), (WIDE, HEIGHT)]
    sizes = [(384, 192), (HEIGHT, 192), (192, 256), (256, 256), (256, HEIGHT)]
    constants = [jax.ShapeDtypeStruct(size, BF) for size in sizes]
    start = call(prior_body, [(WIDE, HEIGHT), *constants], [], 10**8, 10**6, density, halo)
    operands = (near, down, up, got, *start)
    grad, turned, near, far = call(adjoint_body, shapes, scratch, 2 * 10**8, 3 * 10**6, *operands)
    near, far = swap(near, far, "xy")
    whole = jax.ShapeDtypeStruct((HEIGHT, WIDTH), F32)

    def own_part(body, *before):
        return pl.pallas_call(
            body,
            out_shape=[whole, whole, jax.ShapeDtypeStruct((2 * RADIUS, WIDTH), F32)],
            in_specs=[VMEM] * 2 + [HBM] * len(before),
            out_specs=[HBM, HBM, VMEM],
            scratch_shapes=[
                pltpu.VMEM((HEIGHT, WIDTH), F32),
                pltpu.VMEM((HEIGHT - 2 * RADIUS, WIDTH), F32),
                pltpu.SemaphoreType.DMA((2,)),
            ],
            input_output_aliases={2 + index: index for index in range(len(before))},
            compiler_params=pltpu.CompilerParams(vmem_limit_bytes=LIMIT),
            cost_estimate=pl.CostEstimate(flops=10**8, bytes_accessed=10**6, transcendentals=0),
        )(grad, turned, *before)

    own, result, partial_odd = own_part(emit_odd)
    own, result, partial_even = own_part(emit_even, own, result)
    result = pl.pallas_call(
        last_body,
        name="last",
        out_shape=whole,
        in_specs=[VMEM] * 4 + [HBM],
        out_specs=HBM,
        scratch_shapes=[pltpu.VMEM((2, RADIUS, WIDTH), F32), pltpu.SemaphoreType.DMA((2,))],
        input_output_aliases={4: 0},
        compiler_params=pltpu.CompilerParams(vmem_limit_bytes=LIMIT),
        cost_estimate=pl.CostEstimate(flops=10**7, bytes_accessed=10**6, transcendentals=0),
    )(near, far, partial_odd, partial_even, result)
    return (own, result)


def solution(mesh):
    return jax.shard_map(
        steps,
        mesh=mesh,
        in_specs=(P("xy", "gz"), P(None, "gz", "xy", None), P("gz"), P("gz"), P()),
        out_specs=(P("xy", "gz"), P("xy", "gz")),
        check_vma=False,
    )
```

profile of v0, /device:TPU:14, one launch (start us, length us, event | category | flops | bytes accessed | tf_op | source)
XLA Modules:
  0.0 68.1 jit_solution(13292342491180091164)
XLA Ops:
  0.6 2.0 %pack.1 = f32[4,224,128]{2,1,0:T(8,128)} custom-call(s32[4]{0:T(128)} %slope_hbm.1, s32[4]{0:T(128)} %block_hbm.1, f32[2,4]{1,0:T(2,128)} %bitcast.3, f32[384,256]{1,0:T(8,128)} %bitcast.2), custom_call_target="tpu_custom_call" | custom-call | flops 1000000 | bytes 1000000 | tf_op jit(solution)/shard_map/pack/pallas_call | solution.py:376
  2.7 5.3 %all-to-all-start = ((f32[4,224,128]{2,1,0:T(8,128)}), f32[4,224,128]{2,1,0:T(8,128)S(1)}, u32[]{:S(2)}, u32[]{:S(2)}) async-start(f32[4,224,128]{2,1,0:T(8,128)} %pack.1), calls=%async_computation | async-start | bytes 917504 | tf_op jit(solution)/shard_map/all_to_all | solution.py:393
  8.0 1.0 %columns.1 = (f32[64,128]{1,0:T(8,128)S(1)}, f32[64,128]{1,0:T(8,128)S(1)}, f32[32,512]{1,0:T(8,128)S(1)}, f32[32,512]{1,0:T(8,128)S(1)}) custom-call(f32[128,512]{1,0:T(8,128)} %own.1), custom_call_target="tpu_custom_call" | custom-call | flops 1000000 | bytes 1000000 | tf_op jit(solution)/shard_map/columns/pallas_call | solution.py:365
  9.0 1.9 %collective-permute-start = (f32[64,128]{1,0:T(8,128)S(1)}, f32[64,128]{1,0:T(8,128)S(1)}, u32[]{:S(2)}, u32[]{:S(2)}) collective-permute-start(f32[64,128]{1,0:T(8,128)S(1)} %get-tuple-element.25), channel_id=1, source_target_pairs={{0,1},{2,3},{1,0},{3,2},{4,5},{6,7},{5,4},{7,6},{8,9},{10,11},{9,8... | collective-permute-start | bytes 98312 | tf_op jit(solution)/shard_map/ppermute | solution.py:360
  11.0 4.8 %collective-permute-start.1 = (f32[64,128]{1,0:T(8,128)S(1)}, f32[64,128]{1,0:T(8,128)S(1)}, u32[]{:S(2)}, u32[]{:S(2)}) collective-permute-start(f32[64,128]{1,0:T(8,128)S(1)} %get-tuple-element.26), channel_id=1, source_target_pairs={{1,2},{2,1},{5,6},{6,5},{9,10},{10,9},{13,14},{14,13},{17,18},{18,... | collective-permute-start | bytes 98312 | tf_op jit(solution)/shard_map/ppermute | solution.py:359
  15.8 0.9 %collective-permute-done.near = f32[64,128]{1,0:T(8,128)S(1)} collective-permute-done((f32[64,128]{1,0:T(8,128)S(1)}, f32[64,128]{1,0:T(8,128)S(1)}, u32[]{:S(2)}, u32[]{:S(2)}) %collective-permute-start) | collective-permute-done | bytes 32800 | tf_op jit(solution)/shard_map/ppermute | solution.py:360
  16.7 3.6 %collective-permute-done.1.far = f32[64,128]{1,0:T(8,128)S(1)} collective-permute-done((f32[64,128]{1,0:T(8,128)S(1)}, f32[64,128]{1,0:T(8,128)S(1)}, u32[]{:S(2)}, u32[]{:S(2)}) %collective-permute-start.1) | collective-permute-done | bytes 32800 | tf_op jit(solution)/shard_map/ppermute | solution.py:359
  20.3 0.1 shard_map.68
  20.4 1.9 %collective-permute-start.2 = (f32[32,640]{1,0:T(8,128)S(1)}, f32[32,640]{1,0:T(8,128)S(1)}, u32[]{:S(2)}, u32[]{:S(2)}) collective-permute-start(f32[32,640]{1,0:T(8,128)S(1)} %get-tuple-element.29), channel_id=1, source_target_pairs={{0,4},{8,12},{16,20},{24,28},{32,36},{40,44},{48,52},{56,60},{64,6... | collective-permute-start | bytes 245768 | tf_op jit(solution)/shard_map/ppermute | solution.py:399
  22.3 15.4 %collective-permute-start.4 = (f32[32,640]{1,0:T(8,128)S(1)}, f32[32,640]{1,0:T(8,128)S(1)}, u32[]{:S(2)}, u32[]{:S(2)}) collective-permute-start(f32[32,640]{1,0:T(8,128)S(1)} %get-tuple-element.30), channel_id=1, source_target_pairs={{8,4},{16,12},{24,20},{32,28},{40,36},{48,44},{56,52},{64,60},{72,... | collective-permute-start | bytes 245768 | tf_op jit(solution)/shard_map/ppermute | solution.py:398
  37.8 1.3 %collective-permute-start.3 = (f32[32,640]{1,0:T(8,128)S(1)}, f32[32,640]{1,0:T(8,128)S(1)}, u32[]{:S(2)}, u32[]{:S(2)}) collective-permute-start(f32[32,640]{1,0:T(8,128)S(1)} %get-tuple-element.30), channel_id=1, source_target_pairs={{4,8},{12,16},{20,24},{28,32},{36,40},{44,48},{52,56},{60,64},{68,... | collective-permute-start | bytes 245768 | tf_op jit(solution)/shard_map/ppermute | solution.py:397
  39.1 0.0 copy-done
  39.1 0.9 %shard_map.69 = (f32[576,128]{1,0:T(8,128)S(1)}, bf16[384,192]{1,0:T(8,128)(2,1)S(1)}, bf16[128,192]{1,0:T(8,128)(2,1)S(1)}, bf16[192,256]{1,0:T(8,128)(2,1)S(1)...) custom-call(f32[128,512]{1,0:T(8,128)S(1)} %copy-done, f32[128,128]{1,0:T(8,128)S(1)} %get-tuple-element.31.halo), custom_call_target="tpu_custom_call" | custom-call | flops 100000000 | bytes 1000000 | tf_op jit(solution)/shard_map/pallas_call | solution.py:56
  40.0 0.0 collective-permute-done.2.near
  40.0 0.0 collective-permute-done.4.up
  40.0 10.4 %collective-permute-done.3.down = f32[32,640]{1,0:T(8,128)S(1)} collective-permute-done((f32[32,640]{1,0:T(8,128)S(1)}, f32[32,640]{1,0:T(8,128)S(1)}, u32[]{:S(2)}, u32[]{:S(2)}) %collective-permute-start.3) | collective-permute-done | bytes 81952 | tf_op jit(solution)/shard_map/ppermute | solution.py:397
  50.5 0.0 all-to-all-done.got
  50.5 2.4 %shard_map.70 = (f32[512,128]{1,0:T(8,128)S(1)}, f32[128,512]{1,0:T(8,128)S(1)}, f32[32,512]{1,0:T(8,128)S(1)}, f32[32,512]{1,0:T(8,128)S(1)}) custom-call(f32[32,640]{1,0:T(8,128)S(1)} %collective-permute-done.2.near, f32[32,640]{1,0:T(8,128)S(1)} %collective-permute-done.3.down, f32[32,640]{1,0:T(8,128)S(1)} %collective-permute-done.4.up, ...), custom_call_target="tpu_custom_call" | custom-call | flops 200000000 | bytes 3000000 | tf_op jit(solution)/shard_map/pallas_call | solution.py:56
  52.8 1.9 %collective-permute-start.5 = (f32[32,512]{1,0:T(8,128)S(1)}, f32[32,512]{1,0:T(8,128)S(1)}, u32[]{:S(2)}, u32[]{:S(2)}) collective-permute-start(f32[32,512]{1,0:T(8,128)S(1)} %get-tuple-element.43), channel_id=1, source_target_pairs={{0,4},{8,12},{16,20},{24,28},{32,36},{40,44},{48,52},{56,60},{64,6... | collective-permute-start | bytes 196616 | tf_op jit(solution)/shard_map/ppermute | solution.py:360
  54.7 1.9 %collective-permute-start.6 = (f32[32,512]{1,0:T(8,128)S(1)}, f32[32,512]{1,0:T(8,128)S(1)}, u32[]{:S(2)}, u32[]{:S(2)}) collective-permute-start(f32[32,512]{1,0:T(8,128)S(1)} %get-tuple-element.44), channel_id=1, source_target_pairs={{4,8},{12,16},{20,24},{28,32},{36,40},{44,48},{52,56},{60,64},{68,... | collective-permute-start | bytes 196616 | tf_op jit(solution)/shard_map/ppermute | solution.py:359
  56.7 1.0 %shard_map.72 = (f32[128,512]{1,0:T(8,128)}, f32[128,512]{1,0:T(8,128)}, f32[64,512]{1,0:T(8,128)S(1)}) custom-call(f32[512,128]{1,0:T(8,128)S(1)} %get-tuple-element.38.grad, f32[128,512]{1,0:T(8,128)S(1)} %get-tuple-element.39.turned, f32[128,512]{1,0:T(8,128)} %get-tuple-element.40.out_before, ...), custom_call_target="tpu_custom_call", output_to_operand_aliasing={{0}: (2, {}), {1}: (3, {})} | custom-call | flops 100000000 | bytes 1000000 | tf_op jit(solution)/shard_map/pallas_call | solution.py:411
  57.7 0.0 collective-permute-done.5.near
  57.7 9.5 %collective-permute-done.6.far = f32[32,512]{1,0:T(8,128)S(1)} collective-permute-done((f32[32,512]{1,0:T(8,128)S(1)}, f32[32,512]{1,0:T(8,128)S(1)}, u32[]{:S(2)}, u32[]{:S(2)}) %collective-permute-start.6) | collective-permute-done | bytes 65568 | tf_op jit(solution)/shard_map/ppermute | solution.py:359
  67.2 0.9 %last.1 = f32[128,512]{1,0:T(8,128)} custom-call(f32[32,512]{1,0:T(8,128)S(1)} %collective-permute-done.5.near, f32[32,512]{1,0:T(8,128)S(1)} %collective-permute-done.6.far, f32[64,512]{1,0:T(8,128)S(1)} %get-tuple-element.45.partial_odd, f32[64,512]{1,0:T(8,128)S(1)} %get-tuple-element.46.partial_even, ...), custom_call_target="tpu_custom_call", output_to_operand_aliasing={{}: (4, {})} | custom-call | flops 10000000 | bytes 1000000 | tf_op jit(solution)/shard_map/last/pallas_call | solution.py:428
  (2 shorter events, 0.0 us)
Async XLA Ops:
  2.7 47.8 %all-to-all-start = ((f32[4,224,128]{2,1,0:T(8,128)}), f32[4,224,128]{2,1,0:T(8,128)S(1)}, u32[]{:S(2)}, u32[]{:S(2)}) async-start(f32[4,224,128]{2,1,0:T(8,128)} %pack.1), calls=%async_computation | async-start | bytes 917504 | tf_op jit(solution)/shard_map/all_to_all | solution.py:393
  8.0 31.1 %copy-start = (f32[128,512]{1,0:T(8,128)S(1)}, f32[128,512]{1,0:T(8,128)}, u32[]{:S(2)}) copy-start(f32[128,512]{1,0:T(8,128)} %own.1) | copy-start | bytes 786436
  9.0 7.7 %collective-permute-start = (f32[64,128]{1,0:T(8,128)S(1)}, f32[64,128]{1,0:T(8,128)S(1)}, u32[]{:S(2)}, u32[]{:S(2)}) collective-permute-start(f32[64,128]{1,0:T(8,128)S(1)} %get-tuple-element.25), channel_id=1, source_target_pairs={{0,1},{2,3},{1,0},{3,2},{4,5},{6,7},{5,4},{7,6},{8,9},{10,11},{9,8... | collective-permute-start | bytes 98312 | tf_op jit(solution)/shard_map/ppermute | solution.py:360
  11.0 9.4 %collective-permute-start.1 = (f32[64,128]{1,0:T(8,128)S(1)}, f32[64,128]{1,0:T(8,128)S(1)}, u32[]{:S(2)}, u32[]{:S(2)}) collective-permute-start(f32[64,128]{1,0:T(8,128)S(1)} %get-tuple-element.26), channel_id=1, source_target_pairs={{1,2},{2,1},{5,6},{6,5},{9,10},{10,9},{13,14},{14,13},{17,18},{18,... | collective-permute-start | bytes 98312 | tf_op jit(solution)/shard_map/ppermute | solution.py:359
  20.4 19.6 %collective-permute-start.2 = (f32[32,640]{1,0:T(8,128)S(1)}, f32[32,640]{1,0:T(8,128)S(1)}, u32[]{:S(2)}, u32[]{:S(2)}) collective-permute-start(f32[32,640]{1,0:T(8,128)S(1)} %get-tuple-element.29), channel_id=1, source_target_pairs={{0,4},{8,12},{16,20},{24,28},{32,36},{40,44},{48,52},{56,60},{64,6... | collective-permute-start | bytes 245768 | tf_op jit(solution)/shard_map/ppermute | solution.py:399
  22.3 17.7 %collective-permute-start.4 = (f32[32,640]{1,0:T(8,128)S(1)}, f32[32,640]{1,0:T(8,128)S(1)}, u32[]{:S(2)}, u32[]{:S(2)}) collective-permute-start(f32[32,640]{1,0:T(8,128)S(1)} %get-tuple-element.30), channel_id=1, source_target_pairs={{8,4},{16,12},{24,20},{32,28},{40,36},{48,44},{56,52},{64,60},{72,... | collective-permute-start | bytes 245768 | tf_op jit(solution)/shard_map/ppermute | solution.py:398
  37.8 12.7 %collective-permute-start.3 = (f32[32,640]{1,0:T(8,128)S(1)}, f32[32,640]{1,0:T(8,128)S(1)}, u32[]{:S(2)}, u32[]{:S(2)}) collective-permute-start(f32[32,640]{1,0:T(8,128)S(1)} %get-tuple-element.30), channel_id=1, source_target_pairs={{4,8},{12,16},{20,24},{28,32},{36,40},{44,48},{52,56},{60,64},{68,... | collective-permute-start | bytes 245768 | tf_op jit(solution)/shard_map/ppermute | solution.py:397
  52.8 4.9 %collective-permute-start.5 = (f32[32,512]{1,0:T(8,128)S(1)}, f32[32,512]{1,0:T(8,128)S(1)}, u32[]{:S(2)}, u32[]{:S(2)}) collective-permute-start(f32[32,512]{1,0:T(8,128)S(1)} %get-tuple-element.43), channel_id=1, source_target_pairs={{0,4},{8,12},{16,20},{24,28},{32,36},{40,44},{48,52},{56,60},{64,6... | collective-permute-start | bytes 196616 | tf_op jit(solution)/shard_map/ppermute | solution.py:360
  54.7 12.5 %collective-permute-start.6 = (f32[32,512]{1,0:T(8,128)S(1)}, f32[32,512]{1,0:T(8,128)S(1)}, u32[]{:S(2)}, u32[]{:S(2)}) collective-permute-start(f32[32,512]{1,0:T(8,128)S(1)} %get-tuple-element.44), channel_id=1, source_target_pairs={{4,8},{12,16},{20,24},{28,32},{36,40},{44,48},{52,56},{60,64},{68,... | collective-permute-start | bytes 196616 | tf_op jit(solution)/shard_map/ppermute | solution.py:359
where the time goes:
time: 68.4 us; the launch traced here: 68.1 us
  starting transfers between devices  34.5 us (50%)
  waiting for transfers between devices  24.4 us (36%)
  Pallas kernels  8.34 us (12%)
  between operations  0.77 us (1%)
    ppermute x1, starting transfers between devices, steps(): up = lax.ppermute(far, 'xy', back(outer))  15.4 us
    ppermute x2, waiting for transfers between devices, swap(): far = lax.ppermute(far, axis, outer + back(outer))  13.1 us
    ppermute x1, waiting for transfers between devices, steps(): down = lax.ppermute(far, 'xy', outer)  10.4 us
    ppermute x2, starting transfers between devices, swap(): far = lax.ppermute(far, axis, outer + back(outer))  6.74 us
    all_to_all x1, starting transfers between devices, steps(): got = lax.all_to_all(send, 'gz', 0, 0, tiled=True)  5.33 us
    ppermute x2, starting transfers between devices, swap(): return (lax.ppermute(near, axis, inner + back(inner)), far)  3.84 us
    pallas_call x3, Pallas kernels, call(): pl.pallas_call(body, out_shape=[out if hasattr(out, 'dtype') else jax.Sha...  3.38 us
    pallas_call x1, Pallas kernels, steps(): pl.pallas_call(pack_body, name='pack', out_shape=[jax.ShapeDtypeStruct((4...  2.02 us
  transfers between devices with their start and end apart: 8, of which 4 were waited for; matrix products, arithmetic and copies ran while one was open for 0% of the time, Pallas kernels for 5%

commit v1 on v0

--- a/solution.py
+++ b/solution.py
@@ -127,24 +127,12 @@
     return iota((1, 128), 1) < 64
 
 
-def columns_body(density, to_near, to_far, rows_near, rows_far, begin, end, sems):
-    first = jnp.where(odd("xy"), 0, HEIGHT - RADIUS)
-    moves = [
-        (density.at[:, pl.ds(0, 128)], begin),
-        (density.at[:, pl.ds(WIDTH - 128, 128)], end),
-        (density.at[pl.ds(pl.multiple_of(first, RADIUS), RADIUS)], rows_near),
-        (density.at[pl.ds(pl.multiple_of(HEIGHT - RADIUS - first, RADIUS), RADIUS)], rows_far),
-    ]
-    copies = [pltpu.make_async_copy(source, target, sems.at[index]) for index, (source, target) in enumerate(moves)]
-    for copy in copies:
-        copy.start()
-    copies[0].wait()
-    copies[1].wait()
-    first = jnp.where(low_lanes(), begin[:64, :], pltpu.roll(begin[64:, :], 64, 1))
-    last = jnp.where(low_lanes(), pltpu.roll(end[:64, :], 64, 1), end[64:, :])
+def columns_body(own, to_near, to_far, rows_near, rows_far):
+    begin, end = (own[:, :128], own[:, WIDTH - 128 :])
+    first = jnp.where(low_lanes(), begin[:64], pltpu.roll(begin[64:], 64, 1))
+    last = jnp.where(low_lanes(), pltpu.roll(end[:64], 64, 1), end[64:])
     to_near[...], to_far[...] = sides("gz", first, last)
-    copies[2].wait()
-    copies[3].wait()
+    rows_near[...], rows_far[...] = sides("xy", own[:RADIUS], own[HEIGHT - RADIUS :])
 
 
 def edges_body(near, far, rows_near, rows_far, halo, to_near, to_far):
@@ -362,16 +350,7 @@
 
 def steps(density, cotangent, slope, layer_block, block_eps):
     shapes = [(64, 128), (64, 128), (RADIUS, WIDTH), (RADIUS, WIDTH)]
-    near, far, *rows = pl.pallas_call(
-        columns_body,
-        name="columns",
-        out_shape=[jax.ShapeDtypeStruct(shape, F32) for shape in shapes],
-        in_specs=[HBM],
-        out_specs=[VMEM] * 4,
-        scratch_shapes=[pltpu.VMEM((HEIGHT, 128), F32), pltpu.VMEM((HEIGHT, 128), F32), pltpu.SemaphoreType.DMA((4,))],
-        compiler_params=pltpu.CompilerParams(vmem_limit_bytes=8 << 20),
-        cost_estimate=pl.CostEstimate(flops=10**6, bytes_accessed=10**6, transcendentals=0),
-    )(pltpu.with_memory_space_constraint(density, pltpu.HBM))
+    near, far, *rows = call(columns_body, shapes, [], 10**5, 10**6, density)
     near, far = swap(near, far, "gz")
     (send,) = pl.pallas_call(
         pack_body,
@@ -398,7 +377,7 @@
     up = lax.ppermute(far, "xy", back(outer))
     near = lax.ppermute(near, "xy", inner + back(inner))
     shapes = [(WIDTH, HEIGHT), (HEIGHT, WIDTH), (RADIUS, WIDTH), (RADIUS, WIDTH)]
-    scratch = [(SLOPES, SUB, CELLS, HEIGHT), (1088, 256), (WIDE, HEIGHT)]
+    scratch = [(SLOPES, SUB, CELLS, HEIGHT), (1088, 256), (WIDE + SUB, HEIGHT)]
     sizes = [(384, 192), (HEIGHT, 192), (192, 256), (256, 256), (256, HEIGHT)]
     constants = [jax.ShapeDtypeStruct(size, BF) for size in sizes]
     start = call(prior_body, [(WIDE, HEIGHT), *constants], [], 10**8, 10**6, density, halo)

time: 68.4 us -> 68.6 us (level)
  waiting for transfers between devices: 24.4 us -> 25.4 us
  Pallas kernels: 8.34 us -> 7.36 us
    pallas_call x1 -> x0, Pallas kernels: 1.04 us -> none  [steps(): pl.pallas_call(columns_body, name='columns', out_shape=[jax.ShapeDtypeStr...]
    ppermute x2, waiting for transfers between devices: 0.93 us -> 1.89 us  [swap(): return (lax.ppermute(near, axis, inner + back(inner)), far)]
    pallas_call x3 -> x4, Pallas kernels: 3.38 us -> 3.44 us  [call(): pl.pallas_call(body, out_shape=[out if hasattr(out, 'dtype') else jax.Sha...]
  transfers between devices with their start and end apart: 8 -> 8, of which waited for: 4 -> 4; matrix products, arithmetic and copies ran while one was open for 0% -> 0% of each run, Pallas kernels for 5% -> 3%
where the time goes in v1:
time: 68.6 us; the launch traced here: 68.2 us
  starting transfers between devices  34.7 us (51%)
  waiting for transfers between devices  25.4 us (37%)
  Pallas kernels  7.36 us (11%)
  between operations  0.77 us (1%)
    ppermute x1, starting transfers between devices, steps(): up = lax.ppermute(far, 'xy', back(outer))  15.4 us
    ppermute x2, waiting for transfers between devices, swap(): far = lax.ppermute(far, axis, outer + back(outer))  13.1 us
    ppermute x1, waiting for transfers between devices, steps(): down = lax.ppermute(far, 'xy', outer)  10.4 us
    ppermute x2, starting transfers between devices, swap(): far = lax.ppermute(far, axis, outer + back(outer))  6.74 us
    all_to_all x1, starting transfers between devices, steps(): got = lax.all_to_all(send, 'gz', 0, 0, tiled=True)  5.46 us
    ppermute x2, starting transfers between devices, swap(): return (lax.ppermute(near, axis, inner + back(inner)), far)  3.84 us
    pallas_call x4, Pallas kernels, call(): pl.pallas_call(body, out_shape=[out if hasattr(out, 'dtype') else jax.Sha...  3.44 us
    pallas_call x1, Pallas kernels, steps(): pl.pallas_call(pack_body, name='pack', out_shape=[jax.ShapeDtypeStruct((4...  2.02 us
  transfers between devices with their start and end apart: 8, of which 4 were waited for; matrix products, arithmetic and copies ran while one was open for 0% of the time, Pallas kernels for 3%

profile of v1, /device:TPU:14, one launch (start us, length us, event | category | flops | bytes accessed | tf_op | source)
XLA Modules:
  0.0 68.2 jit_solution(14366321396338976503)
XLA Ops:
  0.6 2.0 %pack.1 = f32[4,224,128]{2,1,0:T(8,128)} custom-call(s32[4]{0:T(128)} %slope_hbm.1, s32[4]{0:T(128)} %block_hbm.1, f32[2,4]{1,0:T(2,128)} %bitcast.3, f32[384,256]{1,0:T(8,128)} %bitcast.2), custom_call_target="tpu_custom_call" | custom-call | flops 1000000 | bytes 1000000 | tf_op jit(solution)/shard_map/pack/pallas_call | solution.py:355
  2.7 0.0 copy-start
  2.7 5.5 %all-to-all-start = ((f32[4,224,128]{2,1,0:T(8,128)}), f32[4,224,128]{2,1,0:T(8,128)S(1)}, u32[]{:S(2)}, u32[]{:S(2)}) async-start(f32[4,224,128]{2,1,0:T(8,128)} %pack.1), calls=%async_computation | async-start | bytes 917504 | tf_op jit(solution)/shard_map/all_to_all | solution.py:372
  8.1 0.1 shard_map.68
  8.2 1.9 %collective-permute-start = (f32[64,128]{1,0:T(8,128)S(1)}, f32[64,128]{1,0:T(8,128)S(1)}, u32[]{:S(2)}, u32[]{:S(2)}) collective-permute-start(f32[64,128]{1,0:T(8,128)S(1)} %get-tuple-element.25), channel_id=1, source_target_pairs={{0,1},{2,3},{1,0},{3,2},{4,5},{6,7},{5,4},{7,6},{8,9},{10,11},{9,8... | collective-permute-start | bytes 98312 | tf_op jit(solution)/shard_map/ppermute | solution.py:348
  10.2 4.8 %collective-permute-start.1 = (f32[64,128]{1,0:T(8,128)S(1)}, f32[64,128]{1,0:T(8,128)S(1)}, u32[]{:S(2)}, u32[]{:S(2)}) collective-permute-start(f32[64,128]{1,0:T(8,128)S(1)} %get-tuple-element.26), channel_id=1, source_target_pairs={{1,2},{2,1},{5,6},{6,5},{9,10},{10,9},{13,14},{14,13},{17,18},{18,... | collective-permute-start | bytes 98312 | tf_op jit(solution)/shard_map/ppermute | solution.py:347
  15.0 1.9 %collective-permute-done.near = f32[64,128]{1,0:T(8,128)S(1)} collective-permute-done((f32[64,128]{1,0:T(8,128)S(1)}, f32[64,128]{1,0:T(8,128)S(1)}, u32[]{:S(2)}, u32[]{:S(2)}) %collective-permute-start) | collective-permute-done | bytes 32800 | tf_op jit(solution)/shard_map/ppermute | solution.py:348
  16.9 3.6 %collective-permute-done.1.far = f32[64,128]{1,0:T(8,128)S(1)} collective-permute-done((f32[64,128]{1,0:T(8,128)S(1)}, f32[64,128]{1,0:T(8,128)S(1)}, u32[]{:S(2)}, u32[]{:S(2)}) %collective-permute-start.1) | collective-permute-done | bytes 32800 | tf_op jit(solution)/shard_map/ppermute | solution.py:347
  20.5 0.1 shard_map.69
  20.6 1.9 %collective-permute-start.2 = (f32[32,640]{1,0:T(8,128)S(1)}, f32[32,640]{1,0:T(8,128)S(1)}, u32[]{:S(2)}, u32[]{:S(2)}) collective-permute-start(f32[32,640]{1,0:T(8,128)S(1)} %get-tuple-element.29), channel_id=1, source_target_pairs={{0,4},{8,12},{16,20},{24,28},{32,36},{40,44},{48,52},{56,60},{64,6... | collective-permute-start | bytes 245768 | tf_op jit(solution)/shard_map/ppermute | solution.py:378
  22.5 15.4 %collective-permute-start.4 = (f32[32,640]{1,0:T(8,128)S(1)}, f32[32,640]{1,0:T(8,128)S(1)}, u32[]{:S(2)}, u32[]{:S(2)}) collective-permute-start(f32[32,640]{1,0:T(8,128)S(1)} %get-tuple-element.30), channel_id=1, source_target_pairs={{8,4},{16,12},{24,20},{32,28},{40,36},{48,44},{56,52},{64,60},{72,... | collective-permute-start | bytes 245768 | tf_op jit(solution)/shard_map/ppermute | solution.py:377
  37.9 1.3 %collective-permute-start.3 = (f32[32,640]{1,0:T(8,128)S(1)}, f32[32,640]{1,0:T(8,128)S(1)}, u32[]{:S(2)}, u32[]{:S(2)}) collective-permute-start(f32[32,640]{1,0:T(8,128)S(1)} %get-tuple-element.30), channel_id=1, source_target_pairs={{4,8},{12,16},{20,24},{28,32},{36,40},{44,48},{52,56},{60,64},{68,... | collective-permute-start | bytes 245768 | tf_op jit(solution)/shard_map/ppermute | solution.py:376
  39.2 0.9 %shard_map.70 = (f32[576,128]{1,0:T(8,128)S(1)}, bf16[384,192]{1,0:T(8,128)(2,1)S(1)}, bf16[128,192]{1,0:T(8,128)(2,1)S(1)}, bf16[192,256]{1,0:T(8,128)(2,1)S(1)...) custom-call(f32[128,512]{1,0:T(8,128)S(1)} %copy-done, f32[128,128]{1,0:T(8,128)S(1)} %get-tuple-element.31.halo), custom_call_target="tpu_custom_call" | custom-call | flops 100000000 | bytes 1000000 | tf_op jit(solution)/shard_map/pallas_call | solution.py:56
  40.1 0.0 collective-permute-done.2.near
  40.2 0.0 collective-permute-done.4.up
  40.2 10.4 %collective-permute-done.3.down = f32[32,640]{1,0:T(8,128)S(1)} collective-permute-done((f32[32,640]{1,0:T(8,128)S(1)}, f32[32,640]{1,0:T(8,128)S(1)}, u32[]{:S(2)}, u32[]{:S(2)}) %collective-permute-start.3) | collective-permute-done | bytes 81952 | tf_op jit(solution)/shard_map/ppermute | solution.py:376
  50.6 0.0 all-to-all-done.got
  50.6 2.4 %shard_map.71 = (f32[512,128]{1,0:T(8,128)S(1)}, f32[128,512]{1,0:T(8,128)S(1)}, f32[32,512]{1,0:T(8,128)S(1)}, f32[32,512]{1,0:T(8,128)S(1)}) custom-call(f32[32,640]{1,0:T(8,128)S(1)} %collective-permute-done.2.near, f32[32,640]{1,0:T(8,128)S(1)} %collective-permute-done.3.down, f32[32,640]{1,0:T(8,128)S(1)} %collective-permute-done.4.up, ...), custom_call_target="tpu_custom_call" | custom-call | flops 200000000 | bytes 3000000 | tf_op jit(solution)/shard_map/pallas_call | solution.py:56
  53.0 1.9 %collective-permute-start.5 = (f32[32,512]{1,0:T(8,128)S(1)}, f32[32,512]{1,0:T(8,128)S(1)}, u32[]{:S(2)}, u32[]{:S(2)}) collective-permute-start(f32[32,512]{1,0:T(8,128)S(1)} %get-tuple-element.43), channel_id=1, source_target_pairs={{0,4},{8,12},{16,20},{24,28},{32,36},{40,44},{48,52},{56,60},{64,6... | collective-permute-start | bytes 196616 | tf_op jit(solution)/shard_map/ppermute | solution.py:348
  54.9 1.9 %collective-permute-start.6 = (f32[32,512]{1,0:T(8,128)S(1)}, f32[32,512]{1,0:T(8,128)S(1)}, u32[]{:S(2)}, u32[]{:S(2)}) collective-permute-start(f32[32,512]{1,0:T(8,128)S(1)} %get-tuple-element.44), channel_id=1, source_target_pairs={{4,8},{12,16},{20,24},{28,32},{36,40},{44,48},{52,56},{60,64},{68,... | collective-permute-start | bytes 196616 | tf_op jit(solution)/shard_map/ppermute | solution.py:347
  56.9 1.0 %shard_map.73 = (f32[128,512]{1,0:T(8,128)}, f32[128,512]{1,0:T(8,128)}, f32[64,512]{1,0:T(8,128)S(1)}) custom-call(f32[512,128]{1,0:T(8,128)S(1)} %get-tuple-element.38.grad, f32[128,512]{1,0:T(8,128)S(1)} %get-tuple-element.39.turned, f32[128,512]{1,0:T(8,128)} %get-tuple-element.40.out_before, ...), custom_call_target="tpu_custom_call", output_to_operand_aliasing={{0}: (2, {}), {1}: (3, {})} | custom-call | flops 100000000 | bytes 1000000 | tf_op jit(solution)/shard_map/pallas_call | solution.py:390
  57.9 0.0 collective-permute-done.5.near
  57.9 9.5 %collective-permute-done.6.far = f32[32,512]{1,0:T(8,128)S(1)} collective-permute-done((f32[32,512]{1,0:T(8,128)S(1)}, f32[32,512]{1,0:T(8,128)S(1)}, u32[]{:S(2)}, u32[]{:S(2)}) %collective-permute-start.6) | collective-permute-done | bytes 65568 | tf_op jit(solution)/shard_map/ppermute | solution.py:347
  67.4 0.9 %last.1 = f32[128,512]{1,0:T(8,128)} custom-call(f32[32,512]{1,0:T(8,128)S(1)} %collective-permute-done.5.near, f32[32,512]{1,0:T(8,128)S(1)} %collective-permute-done.6.far, f32[64,512]{1,0:T(8,128)S(1)} %get-tuple-element.45.partial_odd, f32[64,512]{1,0:T(8,128)S(1)} %get-tuple-element.46.partial_even, ...), custom_call_target="tpu_custom_call", output_to_operand_aliasing={{}: (4, {})} | custom-call | flops 10000000 | bytes 1000000 | tf_op jit(solution)/shard_map/last/pallas_call | solution.py:407
  (2 shorter events, 0.0 us)
Async XLA Ops:
  2.7 5.5 %copy-start = (f32[128,512]{1,0:T(8,128)S(1)}, f32[128,512]{1,0:T(8,128)}, u32[]{:S(2)}) copy-start(f32[128,512]{1,0:T(8,128)} %own.3) | copy-start | bytes 786436
  2.7 47.9 %all-to-all-start = ((f32[4,224,128]{2,1,0:T(8,128)}), f32[4,224,128]{2,1,0:T(8,128)S(1)}, u32[]{:S(2)}, u32[]{:S(2)}) async-start(f32[4,224,128]{2,1,0:T(8,128)} %pack.1), calls=%async_computation | async-start | bytes 917504 | tf_op jit(solution)/shard_map/all_to_all | solution.py:372
  8.2 8.6 %collective-permute-start = (f32[64,128]{1,0:T(8,128)S(1)}, f32[64,128]{1,0:T(8,128)S(1)}, u32[]{:S(2)}, u32[]{:S(2)}) collective-permute-start(f32[64,128]{1,0:T(8,128)S(1)} %get-tuple-element.25), channel_id=1, source_target_pairs={{0,1},{2,3},{1,0},{3,2},{4,5},{6,7},{5,4},{7,6},{8,9},{10,11},{9,8... | collective-permute-start | bytes 98312 | tf_op jit(solution)/shard_map/ppermute | solution.py:348
  10.2 10.3 %collective-permute-start.1 = (f32[64,128]{1,0:T(8,128)S(1)}, f32[64,128]{1,0:T(8,128)S(1)}, u32[]{:S(2)}, u32[]{:S(2)}) collective-permute-start(f32[64,128]{1,0:T(8,128)S(1)} %get-tuple-element.26), channel_id=1, source_target_pairs={{1,2},{2,1},{5,6},{6,5},{9,10},{10,9},{13,14},{14,13},{17,18},{18,... | collective-permute-start | bytes 98312 | tf_op jit(solution)/shard_map/ppermute | solution.py:347
  20.6 19.6 %collective-permute-start.2 = (f32[32,640]{1,0:T(8,128)S(1)}, f32[32,640]{1,0:T(8,128)S(1)}, u32[]{:S(2)}, u32[]{:S(2)}) collective-permute-start(f32[32,640]{1,0:T(8,128)S(1)} %get-tuple-element.29), channel_id=1, source_target_pairs={{0,4},{8,12},{16,20},{24,28},{32,36},{40,44},{48,52},{56,60},{64,6... | collective-permute-start | bytes 245768 | tf_op jit(solution)/shard_map/ppermute | solution.py:378
  22.5 17.7 %collective-permute-start.4 = (f32[32,640]{1,0:T(8,128)S(1)}, f32[32,640]{1,0:T(8,128)S(1)}, u32[]{:S(2)}, u32[]{:S(2)}) collective-permute-start(f32[32,640]{1,0:T(8,128)S(1)} %get-tuple-element.30), channel_id=1, source_target_pairs={{8,4},{16,12},{24,20},{32,28},{40,36},{48,44},{56,52},{64,60},{72,... | collective-permute-start | bytes 245768 | tf_op jit(solution)/shard_map/ppermute | solution.py:377
  37.9 12.7 %collective-permute-start.3 = (f32[32,640]{1,0:T(8,128)S(1)}, f32[32,640]{1,0:T(8,128)S(1)}, u32[]{:S(2)}, u32[]{:S(2)}) collective-permute-start(f32[32,640]{1,0:T(8,128)S(1)} %get-tuple-element.30), channel_id=1, source_target_pairs={{4,8},{12,16},{20,24},{28,32},{36,40},{44,48},{52,56},{60,64},{68,... | collective-permute-start | bytes 245768 | tf_op jit(solution)/shard_map/ppermute | solution.py:376
  53.0 4.9 %collective-permute-start.5 = (f32[32,512]{1,0:T(8,128)S(1)}, f32[32,512]{1,0:T(8,128)S(1)}, u32[]{:S(2)}, u32[]{:S(2)}) collective-permute-start(f32[32,512]{1,0:T(8,128)S(1)} %get-tuple-element.43), channel_id=1, source_target_pairs={{0,4},{8,12},{16,20},{24,28},{32,36},{40,44},{48,52},{56,60},{64,6... | collective-permute-start | bytes 196616 | tf_op jit(solution)/shard_map/ppermute | solution.py:348
  54.9 12.5 %collective-permute-start.6 = (f32[32,512]{1,0:T(8,128)S(1)}, f32[32,512]{1,0:T(8,128)S(1)}, u32[]{:S(2)}, u32[]{:S(2)}) collective-permute-start(f32[32,512]{1,0:T(8,128)S(1)} %get-tuple-element.44), channel_id=1, source_target_pairs={{4,8},{12,16},{20,24},{28,32},{36,40},{44,48},{52,56},{60,64},{68,... | collective-permute-start | bytes 196616 | tf_op jit(solution)/shard_map/ppermute | solution.py:347
